TPU v7x, 128 devices: a whole 4x4x4 slice. The times are simulated.
128 devices in a mesh: dom: 16 (over y, z), sub: 8 (over x, core).
Axes of the slice: x: 4, y: 4, z: 4, core: 2. Of those that a mesh axis runs over, the one named last changes fastest.
Arguments:
- features: bfloat16 [131072, 256], P(('dom', 'sub')), may hold values from -6 to 6
- cotangent: bfloat16 [131072, 256], P(('dom', 'sub')), may hold values from -6 to 6
- w_self_one: bfloat16 [256, 256], replicated, may hold values from -0.375 to 0.375
- w_nbr_one: bfloat16 [256, 256], replicated, may hold values from -0.375 to 0.375
- bias_one: float32 [256], replicated, may hold values from -4 to 4
- w_self_two: bfloat16 [256, 256], replicated, may hold values from -0.375 to 0.375
- w_nbr_two: bfloat16 [256, 256], replicated, may hold values from -0.375 to 0.375
- in_count: int32 [131072], P(('dom', 'sub')), may hold values from 0 to 7
- send_list: int32 [128, 128, 4], P(('dom', 'sub')), may hold values from 0 to 1023
- src_slot: int32 [128, 2048], P(('dom', 'sub')), may hold values from 0 to 1535
- dst_slot: int32 [128, 2048], P(('dom', 'sub')), may hold values from 0 to 1535
- edge_count: int32 [128], P(('dom', 'sub')), may hold values from 512 to 2048, as said below
Outputs:
- grad_features: bfloat16 [131072, 256], P(('dom', 'sub'))
- grad_weights: float32 [4, 256, 256], replicated
- grad_bias: float32 [256], replicated
Inputs may be any that keep to these rules, and one draw needn't show every extreme that they name: Each device's first edge_count slots are live; one device has all 2048 live in every draw.
All inputs are finite; a program needn't handle non-finite values.
Results may differ from a plain program's by a relative error of at most 0.0056.
Values may be sent and summed in bfloat16 or wider, within the bound.
A program may use at most 64 MiB of HBM per device.

v0:
```python
import math
import jax
import jax.numpy as jnp
from jax import lax
from jax.sharding import PartitionSpec as P


def to_mirrors(master_rows, send_list):
    picked_rows = jnp.take(master_rows, send_list[0], axis=0)
    feature_dim = master_rows.shape[1]
    received = lax.all_to_all(picked_rows, ("dom", "sub"), split_axis=0, concat_axis=0, tiled=True)
    return received.reshape(-1, feature_dim)


def to_masters(mirror_partial, send_list, node_dev):
    feature_dim = mirror_partial.shape[1]
    per_peer = send_list.shape[2]
    sectioned_rows = mirror_partial.reshape(-1, per_peer, feature_dim)
    received = lax.all_to_all(
        sectioned_rows, ("dom", "sub"), split_axis=0, concat_axis=0, tiled=True
    )
    flat_rows = received.reshape(-1, feature_dim)
    owners = send_list[0].reshape(-1)
    placing = (jnp.arange(node_dev, dtype=jnp.int32)[:, None] == owners[None, :]).astype(
        jnp.float32
    )
    return jnp.dot(
        placing, flat_rows, precision=lax.Precision.HIGHEST, preferred_element_type=jnp.float32
    )


def spread(slot_table, from_slot, into_slot, live_count):
    slot_total = slot_table.shape[0]
    edge_slots = from_slot.shape[0]
    feature_dim = slot_table.shape[1]
    block_rows = math.gcd(512, edge_slots)
    slot_ids = jnp.arange(slot_total, dtype=jnp.int32)[None, :]

    def one_block(turn_index, total):
        offset = turn_index * block_rows
        from_part = lax.dynamic_slice_in_dim(from_slot, offset, block_rows)
        into_part = lax.dynamic_slice_in_dim(into_slot, offset, block_rows)
        live_rows = (jnp.arange(block_rows, dtype=jnp.int32) + offset < live_count)[:, None]
        picking = ((from_part[:, None] == slot_ids) & live_rows).astype(slot_table.dtype)
        picked_rows = jnp.dot(picking, slot_table, preferred_element_type=jnp.float32).astype(
            slot_table.dtype
        )
        placing = (into_part[:, None] == slot_ids).astype(slot_table.dtype)
        return total + tdot(placing, picked_rows)

    start_total = jnp.zeros((slot_total, feature_dim), jnp.float32)
    block_count = edge_slots // block_rows
    return lax.fori_loop(0, block_count, one_block, start_total)


def tdot(left, right):
    return lax.dot_general(
        left, right, (((0,), (0,)), ((), ())), preferred_element_type=jnp.float32
    )


def dot_transposed(left, right):
    return lax.dot_general(
        left, right, (((1,), (1,)), ((), ())), preferred_element_type=jnp.float32
    )


def silu_grad(value):
    sigmoid_v = jax.nn.sigmoid(value)
    return sigmoid_v * (1.0 + value * (1.0 - sigmoid_v))


def shards(
    features,
    cotangent,
    w_self_one,
    w_nbr_one,
    bias_one,
    w_self_two,
    w_nbr_two,
    in_count,
    send_list,
    src_slot,
    dst_slot,
    edge_count,
):
    node_dev = features.shape[0]
    sources = src_slot[0]
    targets = dst_slot[0]
    live_count = edge_count[0]
    inverse = (1.0 / jnp.maximum(in_count, 1).astype(jnp.float32))[:, None]

    def gather_sum(master_rows, from_slot, into_slot):
        slot_table = jnp.concatenate([master_rows, to_mirrors(master_rows, send_list)], axis=0)
        partial_value = spread(slot_table, from_slot, into_slot, live_count)
        return partial_value[:node_dev] + to_masters(partial_value[node_dev:], send_list, node_dev)

    mean_one = (gather_sum(features, sources, targets) * inverse).astype(jnp.bfloat16)
    z_one = (
        jnp.dot(features, w_self_one, preferred_element_type=jnp.float32)
        + jnp.dot(mean_one, w_nbr_one, preferred_element_type=jnp.float32)
        + bias_one
    )
    h_one = jax.nn.silu(z_one).astype(jnp.bfloat16)
    message_two = (dot_transposed(cotangent, w_nbr_two) * inverse).astype(jnp.bfloat16)
    forward_sum = gather_sum(h_one, sources, targets)
    backward_sum = gather_sum(message_two, targets, sources)
    mean_two = (forward_sum * inverse).astype(jnp.bfloat16)
    late_self = tdot(h_one, cotangent)
    late_nbr = tdot(mean_two, cotangent)
    grad_h_one = dot_transposed(cotangent, w_self_two) + backward_sum
    grad_z_one = (grad_h_one * silu_grad(z_one)).astype(jnp.bfloat16)
    message_one = (dot_transposed(grad_z_one, w_nbr_one) * inverse).astype(jnp.bfloat16)
    early_self = tdot(features, grad_z_one)
    early_nbr = tdot(mean_one, grad_z_one)
    early_bias = jnp.sum(grad_z_one.astype(jnp.float32), axis=0)
    grad_features = (
        dot_transposed(grad_z_one, w_self_one) + gather_sum(message_one, targets, sources)
    ).astype(jnp.bfloat16)
    self_one, nbr_one, bias_sum, self_two, nbr_two = lax.psum(
        (early_self, early_nbr, early_bias, late_self, late_nbr), ("dom", "sub")
    )
    norm_factor = jnp.float32(node_dev * lax.axis_size("dom") * lax.axis_size("sub")) ** (-0.5)
    grad_weights = jnp.stack([self_one, nbr_one, self_two, nbr_two]) * norm_factor
    grad_bias = bias_sum * norm_factor
    return (grad_features, grad_weights, grad_bias)


def solution(mesh):
    return jax.shard_map(
        shards,
        mesh=mesh,
        in_specs=(
            P(("dom", "sub"), None),
            P(("dom", "sub"), None),
            P(),
            P(),
            P(),
            P(),
            P(),
            P(("dom", "sub")),
            P(("dom", "sub"), None, None),
            P(("dom", "sub"), None),
            P(("dom", "sub"), None),
            P(("dom", "sub")),
        ),
        out_specs=(P(("dom", "sub"), None), P(), P()),
        check_vma=False,
    )
```

profile of v0, /device:TPU:1, one launch (start us, length us, event | category | flops | bytes accessed | tf_op | source)
XLA Modules:
  0.0 453.2 jit_solution(3980596526978102994)
XLA Ops:
  16.2 11.9 %all-to-all-start = ((bf16[128,4,256]{2,1,0:T(4,128)(2,1)}), bf16[128,4,256]{2,1,0:T(4,128)(2,1)}, u32[]{:S(2)}, u32[]{:S(2)}) async-start(bf16[128,4,256]{2,1,0:T(4,128)(2,1)} %get-tuple-element.741), calls=%async_computation | async-start | bytes 524288 | tf_op jit(solution)/shard_map/all_to_all | solution.py:11
  29.0 9.7 %all-to-all-done = bf16[128,4,256]{2,1,0:T(4,128)(2,1)} async-done(((bf16[128,4,256]{2,1,0:T(4,128)(2,1)}), bf16[128,4,256]{2,1,0:T(4,128)(2,1)}, u32[]{:S(2)}, u32[]{:S(2)}) %all-to-all-start) | async-done | bytes 262176 | tf_op jit(solution)/shard_map/all_to_all | solution.py:11
  38.7 4.6 %all-to-all-start.2 = ((bf16[128,4,256]{2,1,0:T(4,128)(2,1)}), bf16[128,4,256]{2,1,0:T(4,128)(2,1)S(1)}, u32[]{:S(2)}, u32[]{:S(2)}) async-start(bf16[128,4,256]{2,1,0:T(4,128)(2,1)} %get-tuple-element.740), calls=%async_computation.2 | async-start | bytes 524288 | tf_op jit(solution)/shard_map/all_to_all | solution.py:11
  46.9 20.3 %while.60 = (s32[]{:T(128)}, f32[1536,256]{1,0:T(8,128)S(1)}, s32[2048]{0:T(1024)S(1)}, s32[2048]{0:T(1024)}, s32[]{:T(128)}, /*index=5*/bf16[1536,256]{1,0:T(8,...) while((s32[]{:T(128)}, f32[1536,256]{1,0:T(8,128)S(1)}, s32[2048]{0:T(1024)S(1)}, ...), condition=%wide.region_1.3_spmd.clone.clone, body=%wide.region_0.0_spmd.clone.clone.sunk | while | flops 808584192 | bytes 3945645 | solution.py:53
  68.7 9.8 %all-to-all-start.1 = ((f32[128,4,256]{2,1,0:T(4,128)}), f32[128,4,256]{2,1,0:T(4,128)S(1)}, u32[]{:S(2)}, u32[]{:S(2)}) async-start(f32[128,4,256]{2,1,0:T(4,128)} %reshape.79), calls=%async_computation.1 | async-start | bytes 1048576 | tf_op jit(solution)/shard_map/all_to_all | solution.py:19
  78.6 22.6 %while.61 = (s32[]{:T(128)}, f32[1536,256]{1,0:T(8,128)}, s32[2048]{0:T(1024)}, s32[2048]{0:T(1024)S(1)}, s32[]{:T(128)}, /*index=5*/bf16[1536,256]{1,0:T(8,128)...) while((s32[]{:T(128)}, f32[1536,256]{1,0:T(8,128)}, s32[2048]{0:T(1024)}, ...), condition=%wide.region_3.5_spmd.clone.clone, body=%wide.region_2.4_spmd.clone.clone.sunk | while | flops 808584192 | bytes 3945645 | solution.py:53
  90.7 4.5 fusion.128
  103.2 9.8 %all-to-all-start.3 = ((f32[128,4,256]{2,1,0:T(4,128)}), f32[128,4,256]{2,1,0:T(4,128)S(1)}, u32[]{:S(2)}, u32[]{:S(2)}) async-start(f32[128,4,256]{2,1,0:T(4,128)} %reshape.82), calls=%async_computation.3 | async-start | bytes 1048576 | tf_op jit(solution)/shard_map/all_to_all | solution.py:19
  117.8 8.8 %all-to-all-done.3 = f32[128,4,256]{2,1,0:T(4,128)S(1)} async-done(((f32[128,4,256]{2,1,0:T(4,128)}), f32[128,4,256]{2,1,0:T(4,128)S(1)}, u32[]{:S(2)}, u32[]{:S(2)}) %all-to-all-start.3) | async-done | bytes 524320 | tf_op jit(solution)/shard_map/all_to_all | solution.py:19
  139.1 4.6 %all-to-all-start.6 = ((bf16[128,4,256]{2,1,0:T(4,128)(2,1)}), bf16[128,4,256]{2,1,0:T(4,128)(2,1)S(1)}, u32[]{:S(2)}, u32[]{:S(2)}) async-start(bf16[128,4,256]{2,1,0:T(4,128)(2,1)} %get-tuple-element.738), calls=%async_computation.6 | async-start | bytes 524288 | tf_op jit(solution)/shard_map/all_to_all | solution.py:11
  144.8 67.1 %psum.39 = f32[256]{0:T(256)S(1)} all-reduce(f32[256]{0:T(256)S(1)} %copy-done.15), channel_id=1, replica_groups=mesh['dom'=16,'sub'=8] {'dom','sub'}, use_global_device_ids=true, to_apply=%region_13.15 | all-reduce | flops 256 | bytes 2048 | tf_op jit(solution)/shard_map/psum | solution.py:120
  212.5 4.7 %all-to-all-start.4 = ((bf16[128,4,256]{2,1,0:T(4,128)(2,1)}), bf16[128,4,256]{2,1,0:T(4,128)(2,1)S(1)}, u32[]{:S(2)}, u32[]{:S(2)}) async-start(bf16[128,4,256]{2,1,0:T(4,128)(2,1)} %get-tuple-element.739), calls=%async_computation.4 | async-start | bytes 524288 | tf_op jit(solution)/shard_map/all_to_all | solution.py:11
  218.2 21.7 %while.63 = (s32[]{:T(128)}, f32[1536,256]{1,0:T(8,128)}, s32[2048]{0:T(1024)S(1)}, s32[2048]{0:T(1024)S(1)}, s32[]{:T(128)}, /*index=5*/bf16[1536,256]{1,0:T(8,...) while((s32[]{:T(128)}, f32[1536,256]{1,0:T(8,128)}, s32[2048]{0:T(1024)S(1)}, ...), condition=%wide.region_10.12_spmd.clone.clone, body=%wide.region_9.11_spmd.clone.clone.sunk | while | flops 808584192 | bytes 3945645 | solution.py:53
  224.0 4.7 %fusion.134 = f32[1536,256]{1,0:T(8,128)} fusion(f32[1536,256]{1,0:T(8,128)} %get-tuple-element.995, s32[512]{0:T(512)S(1)} %dynamic_slice.86, bf16[1536,256]{1,0:T(8,128)(2,1)} %get-tuple-element.1009, s32[512]{0:T(512)S(1)} %dynamic_slice.87, pred[512]{0:T(512)(128)(4,1)S(1)} %add_compare_fusion.11, pred[]{:T(512)S(6)} %compare.15), kind=kOutput, calls=%fused_computation.46.clone.1 | convolution fusion | flops 808583168 | bytes 3936769 | tf_op jit(solution)/shard_map/while/body/eval_jaxpr/dot_general | solution.py:57
  229.6 4.7 %fusion.134 = f32[1536,256]{1,0:T(8,128)} fusion(f32[1536,256]{1,0:T(8,128)} %get-tuple-element.995, s32[512]{0:T(512)S(1)} %dynamic_slice.86, bf16[1536,256]{1,0:T(8,128)(2,1)} %get-tuple-element.1009, s32[512]{0:T(512)S(1)} %dynamic_slice.87, pred[512]{0:T(512)(128)(4,1)S(1)} %add_compare_fusion.11, pred[]{:T(512)S(6)} %compare.15), kind=kOutput, calls=%fused_computation.46.clone.1 | convolution fusion | flops 808583168 | bytes 3936769 | tf_op jit(solution)/shard_map/while/body/eval_jaxpr/dot_general | solution.py:57
  235.1 4.7 %fusion.134 = f32[1536,256]{1,0:T(8,128)} fusion(f32[1536,256]{1,0:T(8,128)} %get-tuple-element.995, s32[512]{0:T(512)S(1)} %dynamic_slice.86, bf16[1536,256]{1,0:T(8,128)(2,1)} %get-tuple-element.1009, s32[512]{0:T(512)S(1)} %dynamic_slice.87, pred[512]{0:T(512)(128)(4,1)S(1)} %add_compare_fusion.11, pred[]{:T(512)S(6)} %compare.15), kind=kOutput, calls=%fused_computation.46.clone.1 | convolution fusion | flops 808583168 | bytes 3936769 | tf_op jit(solution)/shard_map/while/body/eval_jaxpr/dot_general | solution.py:57
  241.9 9.8 %all-to-all-start.7 = ((f32[128,4,256]{2,1,0:T(4,128)}), f32[128,4,256]{2,1,0:T(4,128)S(1)}, u32[]{:S(2)}, u32[]{:S(2)}) async-start(f32[128,4,256]{2,1,0:T(4,128)} %reshape.88), calls=%async_computation.7 | async-start | bytes 1048576 | tf_op jit(solution)/shard_map/all_to_all | solution.py:19
  252.7 21.8 %while.62 = (s32[]{:T(128)}, f32[1536,256]{1,0:T(8,128)}, s32[2048]{0:T(1024)S(1)}, s32[2048]{0:T(1024)S(1)}, s32[]{:T(128)}, /*index=5*/bf16[1536,256]{1,0:T(8,...) while((s32[]{:T(128)}, f32[1536,256]{1,0:T(8,128)}, s32[2048]{0:T(1024)S(1)}, ...), condition=%wide.region_5.7_spmd.clone.clone, body=%wide.region_4.6_spmd.clone.clone.sunk | while | flops 808584192 | bytes 3945645 | solution.py:53
  258.6 4.8 %fusion.131 = f32[1536,256]{1,0:T(8,128)} fusion(f32[1536,256]{1,0:T(8,128)} %get-tuple-element.965, s32[512]{0:T(512)S(1)} %dynamic_slice.84, bf16[1536,256]{1,0:T(8,128)(2,1)} %get-tuple-element.979, s32[512]{0:T(512)S(1)} %dynamic_slice.85, pred[512]{0:T(512)(128)(4,1)S(1)} %add_compare_fusion.10, pred[]{:T(512)S(6)} %compare.14), kind=kOutput, calls=%fused_computation.35.clone.1 | convolution fusion | flops 808583168 | bytes 3936769 | tf_op jit(solution)/shard_map/while/body/eval_jaxpr/dot_general | solution.py:57
  264.1 4.8 %fusion.131 = f32[1536,256]{1,0:T(8,128)} fusion(f32[1536,256]{1,0:T(8,128)} %get-tuple-element.965, s32[512]{0:T(512)S(1)} %dynamic_slice.84, bf16[1536,256]{1,0:T(8,128)(2,1)} %get-tuple-element.979, s32[512]{0:T(512)S(1)} %dynamic_slice.85, pred[512]{0:T(512)(128)(4,1)S(1)} %add_compare_fusion.10, pred[]{:T(512)S(6)} %compare.14), kind=kOutput, calls=%fused_computation.35.clone.1 | convolution fusion | flops 808583168 | bytes 3936769 | tf_op jit(solution)/shard_map/while/body/eval_jaxpr/dot_general | solution.py:57
  269.7 4.8 %fusion.131 = f32[1536,256]{1,0:T(8,128)} fusion(f32[1536,256]{1,0:T(8,128)} %get-tuple-element.965, s32[512]{0:T(512)S(1)} %dynamic_slice.84, bf16[1536,256]{1,0:T(8,128)(2,1)} %get-tuple-element.979, s32[512]{0:T(512)S(1)} %dynamic_slice.85, pred[512]{0:T(512)(128)(4,1)S(1)} %add_compare_fusion.10, pred[]{:T(512)S(6)} %compare.14), kind=kOutput, calls=%fused_computation.35.clone.1 | convolution fusion | flops 808583168 | bytes 3936769 | tf_op jit(solution)/shard_map/while/body/eval_jaxpr/dot_general | solution.py:57
  276.5 9.8 %all-to-all-start.5 = ((f32[128,4,256]{2,1,0:T(4,128)}), f32[128,4,256]{2,1,0:T(4,128)S(1)}, u32[]{:S(2)}, u32[]{:S(2)}) async-start(f32[128,4,256]{2,1,0:T(4,128)} %reshape.85), calls=%async_computation.5 | async-start | bytes 1048576 | tf_op jit(solution)/shard_map/all_to_all | solution.py:19
  291.0 8.9 %all-to-all-done.5 = f32[128,4,256]{2,1,0:T(4,128)S(1)} async-done(((f32[128,4,256]{2,1,0:T(4,128)}), f32[128,4,256]{2,1,0:T(4,128)S(1)}, u32[]{:S(2)}, u32[]{:S(2)}) %all-to-all-start.5) | async-done | bytes 524320 | tf_op jit(solution)/shard_map/all_to_all | solution.py:19
  303.5 140.2 %all-reduce.3.cloned.1.call-done = (f32[1,256,256]{1,2,0:T(8,128)}, f32[1,256,256]{1,2,0:T(8,128)}, f32[1,256,256]{1,2,0:T(8,128)}, f32[1,256,256]{1,2,0:T(8,128)}) async-done(((f32[1,256,256]{1,2,0:T(8,128)}, f32[1,256,256]{1,2,0:T(8,128)}, f32[1,256,256]{1,2,0:T(8,128)}, f32[1,256,256]{1,2,0:T(8,128)}), (f32[1,256,256]{1,2,0:T(8,128)}, f32[1,256,256]{1,2,0:T(8,128)}, f32[1,256,256]{1,2,0:T(8,128)}, ...) | async-done | bytes 1048592 | tf_op jit(solution)/shard_map/psum | solution.py:120
  (158 shorter events, 105.7 us)
Async XLA Ops:
  7.2 2.4 copy-start
  10.8 2.0 copy-start.1
  14.8 13.4 %copy-start.12 = (s32[1,128,4]{1,2,0:T(4,128)S(1)}, s32[1,128,4]{1,2,0:T(4,128)}, u32[]{:S(2)}) copy-start(s32[1,128,4]{1,2,0:T(4,128)} %param.30) | copy-start | bytes 6148
  16.2 30.7 %copy-start.8 = (s32[1,2048]{1,0:T(1,128)S(1)}, s32[1,2048]{1,0:T(1,128)}, u32[]{:S(2)}) copy-start(s32[1,2048]{1,0:T(1,128)} %param.31) | copy-start | bytes 24580
  16.2 22.5 %all-to-all-start = ((bf16[128,4,256]{2,1,0:T(4,128)(2,1)}), bf16[128,4,256]{2,1,0:T(4,128)(2,1)}, u32[]{:S(2)}, u32[]{:S(2)}) async-start(bf16[128,4,256]{2,1,0:T(4,128)(2,1)} %get-tuple-element.741), calls=%async_computation | async-start | bytes 524288 | tf_op jit(solution)/shard_map/all_to_all | solution.py:11
  38.7 29.8 %all-to-all-start.2 = ((bf16[128,4,256]{2,1,0:T(4,128)(2,1)}), bf16[128,4,256]{2,1,0:T(4,128)(2,1)S(1)}, u32[]{:S(2)}, u32[]{:S(2)}) async-start(bf16[128,4,256]{2,1,0:T(4,128)(2,1)} %get-tuple-element.740), calls=%async_computation.2 | async-start | bytes 524288 | tf_op jit(solution)/shard_map/all_to_all | solution.py:11
  67.3 1.4 copy-start.2
  68.7 34.5 %all-to-all-start.1 = ((f32[128,4,256]{2,1,0:T(4,128)}), f32[128,4,256]{2,1,0:T(4,128)S(1)}, u32[]{:S(2)}, u32[]{:S(2)}) async-start(f32[128,4,256]{2,1,0:T(4,128)} %reshape.79), calls=%async_computation.1 | async-start | bytes 1048576 | tf_op jit(solution)/shard_map/all_to_all | solution.py:19
  101.2 11.8 %copy-start.7 = (bf16[256,256]{1,0:T(8,128)(2,1)S(1)}, bf16[256,256]{1,0:T(8,128)(2,1)}, u32[]{:S(2)}) copy-start(bf16[256,256]{1,0:T(8,128)(2,1)} %param.24) | copy-start | bytes 393220
  103.2 23.4 %all-to-all-start.3 = ((f32[128,4,256]{2,1,0:T(4,128)}), f32[128,4,256]{2,1,0:T(4,128)S(1)}, u32[]{:S(2)}, u32[]{:S(2)}) async-start(f32[128,4,256]{2,1,0:T(4,128)} %reshape.82), calls=%async_computation.3 | async-start | bytes 1048576 | tf_op jit(solution)/shard_map/all_to_all | solution.py:19
  113.0 1.5 copy-start.13
  117.8 11.3 %copy-start.4 = (f32[1024,256]{1,0:T(8,128)S(1)}, f32[1024,256]{1,0:T(8,128)}, u32[]{:S(2)}) copy-start(f32[1024,256]{1,0:T(8,128)} %fusion.82) | copy-start | bytes 3145732
  117.8 11.4 %copy-start.11 = (bf16[256,256]{1,0:T(8,128)(2,1)S(1)}, bf16[256,256]{1,0:T(8,128)(2,1)}, u32[]{:S(2)}) copy-start(bf16[256,256]{1,0:T(8,128)(2,1)} %param.25) | copy-start | bytes 393220
  129.2 1.4 copy-start.3
  129.2 1.4 copy-start.16
  137.1 6.6 %copy-start.6 = (bf16[1024,256]{1,0:T(8,128)(2,1)S(1)}, bf16[1024,256]{1,0:T(8,128)(2,1)}, u32[]{:S(2)}) copy-start(bf16[1024,256]{1,0:T(8,128)(2,1)} %copy-done.5) | copy-start | bytes 1572868
  137.2 7.6 %copy-start.15 = (f32[256]{0:T(256)S(1)}, f32[256]{0:T(256)}, u32[]{:S(2)}) copy-start(f32[256]{0:T(256)} %get-tuple-element.744) | copy-start | bytes 3076
  139.1 73.4 %all-to-all-start.6 = ((bf16[128,4,256]{2,1,0:T(4,128)(2,1)}), bf16[128,4,256]{2,1,0:T(4,128)(2,1)S(1)}, u32[]{:S(2)}, u32[]{:S(2)}) async-start(bf16[128,4,256]{2,1,0:T(4,128)(2,1)} %get-tuple-element.738), calls=%async_computation.6 | async-start | bytes 524288 | tf_op jit(solution)/shard_map/all_to_all | solution.py:11
  144.8 73.4 %copy-start.9 = (s32[2048]{0:T(1024)S(1)}, s32[2048]{0:T(1024)}, u32[]{:S(2)}) copy-start(s32[2048]{0:T(1024)} %get-tuple-element.1045) | copy-start | bytes 24580
  212.5 29.4 %all-to-all-start.4 = ((bf16[128,4,256]{2,1,0:T(4,128)(2,1)}), bf16[128,4,256]{2,1,0:T(4,128)(2,1)S(1)}, u32[]{:S(2)}, u32[]{:S(2)}) async-start(bf16[128,4,256]{2,1,0:T(4,128)(2,1)} %get-tuple-element.739), calls=%async_computation.4 | async-start | bytes 524288 | tf_op jit(solution)/shard_map/all_to_all | solution.py:11
  241.9 34.6 %all-to-all-start.7 = ((f32[128,4,256]{2,1,0:T(4,128)}), f32[128,4,256]{2,1,0:T(4,128)S(1)}, u32[]{:S(2)}, u32[]{:S(2)}) async-start(f32[128,4,256]{2,1,0:T(4,128)} %reshape.88), calls=%async_computation.7 | async-start | bytes 1048576 | tf_op jit(solution)/shard_map/all_to_all | solution.py:19
  276.5 11.1 %copy-start.14 = (s32[512]{0:T(512)S(1)}, s32[512]{0:T(512)}, u32[]{:S(2)}) copy-start(s32[512]{0:T(512)} %eq.293) | copy-start | bytes 6148
  276.5 23.4 %all-to-all-start.5 = ((f32[128,4,256]{2,1,0:T(4,128)}), f32[128,4,256]{2,1,0:T(4,128)S(1)}, u32[]{:S(2)}, u32[]{:S(2)}) async-start(f32[128,4,256]{2,1,0:T(4,128)} %reshape.85), calls=%async_computation.5 | async-start | bytes 1048576 | tf_op jit(solution)/shard_map/all_to_all | solution.py:19
  286.3 157.5 %all-reduce.3.cloned.1.call-start = ((), (), s32[]{:S(2)}) async-start(), calls=%async_computation.8 | async-start | bytes 2097152 | tf_op jit(solution)/shard_map/psum | solution.py:120
  (2 other events, 2.5 us)
Sparse Core Ops, SparseCore 0:
  293.1 150.6 all-reduce.2
where the time goes:
time: 455 us; the launch traced here: 453 us
  waiting for transfers between devices  168 us (37%)
  matrix products  88.7 us (19%)
  blocking collectives  67.1 us (15%)
  starting transfers between devices  64.9 us (14%)
  local copies, waits for them, and re-layouts  28.8 us (6%)
  other arithmetic  21.3 us (5%)
  between operations  14.5 us (3%)
    psum x1, waiting for transfers between devices, shards(): lax.psum((early_self, early_nbr, early_bias, late_self, late_nbr), ('dom'...  140 us
    dot_general x20, matrix products, tdot(): lax.dot_general(left, right, (((0,), (0,)), ((), ())), preferred_element_...  72.1 us
    psum x1, blocking collectives, shards(): lax.psum((early_self, early_nbr, early_bias, late_self, late_nbr), ('dom'...  67.1 us
    all_to_all x4, starting transfers between devices, to_masters(): lax.all_to_all(sectioned_rows, ('dom', 'sub'), split_axis=0, concat_axis=...  39.1 us
    all_to_all x4, starting transfers between devices, to_mirrors(): lax.all_to_all(picked_rows, ('dom', 'sub'), split_axis=0, concat_axis=0,...  25.8 us
    all_to_all x4, waiting for transfers between devices, to_masters(): lax.all_to_all(sectioned_rows, ('dom', 'sub'), split_axis=0, concat_axis=...  17.7 us
    lt x16, other arithmetic, one_block(): jnp.arange(block_rows, dtype=jnp.int32) + offset < live_count  10.4 us
    dot_general x4, matrix products, to_masters(): jnp.dot(placing, flat_rows, precision=lax.Precision.HIGHEST, preferred_el...  10.2 us
  transfers between devices with their start and end apart: 9, of which 4 were waited for; matrix products, arithmetic and copies ran while one was open for 25% of the time, Pallas kernels for 0%

commit v1 on v0

--- a/solution.py
+++ b/solution.py
@@ -118,7 +118,7 @@
         dot_transposed(grad_z_one, w_self_one) + gather_sum(message_one, targets, sources)
     ).astype(jnp.bfloat16)
     self_one, nbr_one, bias_sum, self_two, nbr_two = lax.psum(
-        (early_self, early_nbr, early_bias, late_self, late_nbr), ("dom", "sub")
+        lax.psum((early_self, early_nbr, early_bias, late_self, late_nbr), "sub"), "dom"
     )
     norm_factor = jnp.float32(node_dev * lax.axis_size("dom") * lax.axis_size("sub")) ** (-0.5)
     grad_weights = jnp.stack([self_one, nbr_one, self_two, nbr_two]) * norm_factor

time: 455 us -> 375 us (0.82)
  waiting for transfers between devices: 168 us -> 108 us
  blocking collectives: 67.1 us -> 47.8 us
  local copies, waits for them, and re-layouts: 28.8 us -> 34.5 us
  starting transfers between devices: 64.9 us -> 59.8 us
    psum x1 -> x2, waiting for transfers between devices: 140 us -> 70 us  [the longest x1 39.3 us: shards(): lax.psum(lax.psum((early_self, early_nbr, early_bias, late_self, late_nbr...]
    psum x1 -> x2, blocking collectives: 67.1 us -> 47.8 us  [the longest x1 33.5 us: shards(): lax.psum(lax.psum((early_self, early_nbr, early_bias, late_self, late_nbr...]
    all_to_all x4, waiting for transfers between devices: 9.69 us -> 18.6 us  [to_mirrors(): lax.all_to_all(picked_rows, ('dom', 'sub'), split_axis=0, concat_axis=0,...]
    all_to_all x4, starting transfers between devices: 39.1 us -> 33.9 us  [to_masters(): lax.all_to_all(sectioned_rows, ('dom', 'sub'), split_axis=0, concat_axis=...]
  transfers between devices with their start and end apart: 9 -> 10, of which waited for: 4 -> 6; matrix products, arithmetic and copies ran while one was open for 25% -> 31% of each run, Pallas kernels for 0% -> 0%
where the time goes in v1:
time: 375 us; the launch traced here: 372 us
  waiting for transfers between devices  108 us (29%)
  matrix products  85.7 us (23%)
  starting transfers between devices  59.8 us (16%)
  blocking collectives  47.8 us (13%)
  local copies, waits for them, and re-layouts  34.5 us (9%)
  other arithmetic  21.2 us (6%)
  between operations  14.5 us (4%)
    dot_general x20, matrix products, tdot(): lax.dot_general(left, right, (((0,), (0,)), ((), ())), preferred_element_...  68.9 us
    psum x1, waiting for transfers between devices, shards(): lax.psum(lax.psum((early_self, early_nbr, early_bias, late_self, late_nbr...  39.3 us
    all_to_all x4, starting transfers between devices, to_masters(): lax.all_to_all(sectioned_rows, ('dom', 'sub'), split_axis=0, concat_axis=...  33.9 us
    psum x1, blocking collectives, shards(): lax.psum(lax.psum((early_self, early_nbr, early_bias, late_self, late_nbr...  33.5 us
    psum x1, waiting for transfers between devices, shards(): lax.psum((early_self, early_nbr, early_bias, late_self, late_nbr), 'sub')  30.7 us
    all_to_all x4, starting transfers between devices, to_mirrors(): lax.all_to_all(picked_rows, ('dom', 'sub'), split_axis=0, concat_axis=0,...  25.6 us
    all_to_all x4, waiting for transfers between devices, to_masters(): lax.all_to_all(sectioned_rows, ('dom', 'sub'), split_axis=0, concat_axis=...  19.1 us
    all_to_all x4, waiting for transfers between devices, to_mirrors(): lax.all_to_all(picked_rows, ('dom', 'sub'), split_axis=0, concat_axis=0,...  18.6 us
  transfers between devices with their start and end apart: 10, of which 6 were waited for; matrix products, arithmetic and copies ran while one was open for 31% of the time, Pallas kernels for 0%

profile of v1, /device:TPU:1, one launch (start us, length us, event | category | flops | bytes accessed | tf_op | source)
XLA Modules:
  0.0 371.6 jit_solution(474422452261983661)
XLA Ops:
  16.2 11.9 %all-to-all-start = ((bf16[128,4,256]{2,1,0:T(4,128)(2,1)}), bf16[128,4,256]{2,1,0:T(4,128)(2,1)}, u32[]{:S(2)}, u32[]{:S(2)}) async-start(bf16[128,4,256]{2,1,0:T(4,128)(2,1)} %get-tuple-element.745), calls=%async_computation | async-start | bytes 524288 | tf_op jit(solution)/shard_map/all_to_all | solution.py:11
  29.0 9.7 %all-to-all-done = bf16[128,4,256]{2,1,0:T(4,128)(2,1)} async-done(((bf16[128,4,256]{2,1,0:T(4,128)(2,1)}), bf16[128,4,256]{2,1,0:T(4,128)(2,1)}, u32[]{:S(2)}, u32[]{:S(2)}) %all-to-all-start) | async-done | bytes 262176 | tf_op jit(solution)/shard_map/all_to_all | solution.py:11
  38.7 4.6 %all-to-all-start.2 = ((bf16[128,4,256]{2,1,0:T(4,128)(2,1)}), bf16[128,4,256]{2,1,0:T(4,128)(2,1)S(1)}, u32[]{:S(2)}, u32[]{:S(2)}) async-start(bf16[128,4,256]{2,1,0:T(4,128)(2,1)} %get-tuple-element.744), calls=%async_computation.2 | async-start | bytes 524288 | tf_op jit(solution)/shard_map/all_to_all | solution.py:11
  46.9 20.3 %while.60 = (s32[]{:T(128)}, f32[1536,256]{1,0:T(8,128)S(1)}, s32[2048]{0:T(1024)S(1)}, s32[2048]{0:T(1024)}, s32[]{:T(128)}, /*index=5*/bf16[1536,256]{1,0:T(8,...) while((s32[]{:T(128)}, f32[1536,256]{1,0:T(8,128)S(1)}, s32[2048]{0:T(1024)S(1)}, ...), condition=%wide.region_1.3_spmd.clone.clone, body=%wide.region_0.0_spmd.clone.clone.sunk | while | flops 808584192 | bytes 3945645 | solution.py:53
  68.6 9.8 %all-to-all-start.1 = ((f32[128,4,256]{2,1,0:T(4,128)}), f32[128,4,256]{2,1,0:T(4,128)S(1)}, u32[]{:S(2)}, u32[]{:S(2)}) async-start(f32[128,4,256]{2,1,0:T(4,128)} %reshape.79), calls=%async_computation.1 | async-start | bytes 1048576 | tf_op jit(solution)/shard_map/all_to_all | solution.py:19
  78.5 22.7 %while.61 = (s32[]{:T(128)}, f32[1536,256]{1,0:T(8,128)}, s32[2048]{0:T(1024)}, s32[2048]{0:T(1024)S(1)}, s32[]{:T(128)}, /*index=5*/bf16[1536,256]{1,0:T(8,128)...) while((s32[]{:T(128)}, f32[1536,256]{1,0:T(8,128)}, s32[2048]{0:T(1024)}, ...), condition=%wide.region_3.5_spmd.clone.clone, body=%wide.region_2.4_spmd.clone.clone.sunk | while | flops 808584192 | bytes 3945645 | solution.py:53
  84.6 4.5 %fusion.131 = f32[1536,256]{1,0:T(8,128)} fusion(f32[1536,256]{1,0:T(8,128)} %get-tuple-element.909, s32[512]{0:T(512)S(1)} %dynamic_slice.82, bf16[1536,256]{1,0:T(8,128)(2,1)S(1)} %get-tuple-element.923, s32[512]{0:T(512)S(1)} %dynamic_slice.83, pred[512]{0:T(512)(128)(4,1)S(1)} %add_compare_fusion.9, pred[]{:T(512)S(6)} %compare.13), kind=kOutput, calls=%fused_computation.24.clone.1 | convolution fusion | flops 808583168 | bytes 3936769 | tf_op jit(solution)/shard_map/while/body/eval_jaxpr/dot_general | solution.py:57
  90.7 4.5 %fusion.131 = f32[1536,256]{1,0:T(8,128)} fusion(f32[1536,256]{1,0:T(8,128)} %get-tuple-element.909, s32[512]{0:T(512)S(1)} %dynamic_slice.82, bf16[1536,256]{1,0:T(8,128)(2,1)S(1)} %get-tuple-element.923, s32[512]{0:T(512)S(1)} %dynamic_slice.83, pred[512]{0:T(512)(128)(4,1)S(1)} %add_compare_fusion.9, pred[]{:T(512)S(6)} %compare.13), kind=kOutput, calls=%fused_computation.24.clone.1 | convolution fusion | flops 808583168 | bytes 3936769 | tf_op jit(solution)/shard_map/while/body/eval_jaxpr/dot_general | solution.py:57
  103.3 9.8 %all-to-all-start.3 = ((f32[128,4,256]{2,1,0:T(4,128)}), f32[128,4,256]{2,1,0:T(4,128)S(1)}, u32[]{:S(2)}, u32[]{:S(2)}) async-start(f32[128,4,256]{2,1,0:T(4,128)} %reshape.82), calls=%async_computation.3 | async-start | bytes 1048576 | tf_op jit(solution)/shard_map/all_to_all | solution.py:19
  117.8 8.8 %all-to-all-done.3 = f32[128,4,256]{2,1,0:T(4,128)S(1)} async-done(((f32[128,4,256]{2,1,0:T(4,128)}), f32[128,4,256]{2,1,0:T(4,128)S(1)}, u32[]{:S(2)}, u32[]{:S(2)}) %all-to-all-start.3) | async-done | bytes 524320 | tf_op jit(solution)/shard_map/all_to_all | solution.py:19
  138.9 4.6 %all-to-all-start.6 = ((bf16[128,4,256]{2,1,0:T(4,128)(2,1)}), bf16[128,4,256]{2,1,0:T(4,128)(2,1)S(1)}, u32[]{:S(2)}, u32[]{:S(2)}) async-start(bf16[128,4,256]{2,1,0:T(4,128)(2,1)} %get-tuple-element.742), calls=%async_computation.6 | async-start | bytes 524288 | tf_op jit(solution)/shard_map/all_to_all | solution.py:11
  145.7 8.9 %all-to-all-done.6 = bf16[128,4,256]{2,1,0:T(4,128)(2,1)S(1)} async-done(((bf16[128,4,256]{2,1,0:T(4,128)(2,1)}), bf16[128,4,256]{2,1,0:T(4,128)(2,1)S(1)}, u32[]{:S(2)}, u32[]{:S(2)}) %all-to-all-start.6) | async-done | bytes 262176 | tf_op jit(solution)/shard_map/all_to_all | solution.py:11
  160.1 24.4 %while.63 = (s32[]{:T(128)}, f32[1536,256]{1,0:T(8,128)}, s32[2048]{0:T(1024)}, s32[2048]{0:T(1024)S(1)}, s32[]{:T(128)}, /*index=5*/bf16[1536,256]{1,0:T(8,128)(2,1)}, s32[]{:T(128)}, s32[]{:T(128)}, s32[]{:T(128)}, s32[]{:T(128)}) while((s32[]{:T(128)}, f32[1536,256]{1,0:T(8,128)}, s32[2048]{0:T(1024)}, ...), condition=%wide.region_13.15_spmd.clone.clone, body=%wide.region_12.14_spmd.clone.clone.sunk | while | flops 808584192 | bytes 3945645 | solution.py:53
  167.3 4.7 %fusion.137 = f32[1536,256]{1,0:T(8,128)} fusion(f32[1536,256]{1,0:T(8,128)} %get-tuple-element.999, s32[512]{0:T(512)S(1)} %dynamic_slice.86, bf16[1536,256]{1,0:T(8,128)(2,1)} %get-tuple-element.1013, s32[512]{0:T(512)S(1)} %dynamic_slice.87, pred[512]{0:T(512)(128)(4,1)S(1)} %add_compare_fusion.11, pred[]{:T(512)S(6)} %compare.15), kind=kOutput, calls=%fused_computation.46.clone.1 | convolution fusion | flops 808583168 | bytes 3936769 | tf_op jit(solution)/shard_map/while/body/eval_jaxpr/dot_general | solution.py:57
  173.5 4.7 %fusion.137 = f32[1536,256]{1,0:T(8,128)} fusion(f32[1536,256]{1,0:T(8,128)} %get-tuple-element.999, s32[512]{0:T(512)S(1)} %dynamic_slice.86, bf16[1536,256]{1,0:T(8,128)(2,1)} %get-tuple-element.1013, s32[512]{0:T(512)S(1)} %dynamic_slice.87, pred[512]{0:T(512)(128)(4,1)S(1)} %add_compare_fusion.11, pred[]{:T(512)S(6)} %compare.15), kind=kOutput, calls=%fused_computation.46.clone.1 | convolution fusion | flops 808583168 | bytes 3936769 | tf_op jit(solution)/shard_map/while/body/eval_jaxpr/dot_general | solution.py:57
  179.8 4.7 %fusion.137 = f32[1536,256]{1,0:T(8,128)} fusion(f32[1536,256]{1,0:T(8,128)} %get-tuple-element.999, s32[512]{0:T(512)S(1)} %dynamic_slice.86, bf16[1536,256]{1,0:T(8,128)(2,1)} %get-tuple-element.1013, s32[512]{0:T(512)S(1)} %dynamic_slice.87, pred[512]{0:T(512)(128)(4,1)S(1)} %add_compare_fusion.11, pred[]{:T(512)S(6)} %compare.15), kind=kOutput, calls=%fused_computation.46.clone.1 | convolution fusion | flops 808583168 | bytes 3936769 | tf_op jit(solution)/shard_map/while/body/eval_jaxpr/dot_general | solution.py:57
  186.5 9.8 %all-to-all-start.7 = ((f32[128,4,256]{2,1,0:T(4,128)}), f32[128,4,256]{2,1,0:T(4,128)S(1)}, u32[]{:S(2)}, u32[]{:S(2)}) async-start(f32[128,4,256]{2,1,0:T(4,128)} %reshape.88), calls=%async_computation.7 | async-start | bytes 1048576 | tf_op jit(solution)/shard_map/all_to_all | solution.py:19
  199.7 10.2 %all-to-all-done.7 = f32[128,4,256]{2,1,0:T(4,128)S(1)} async-done(((f32[128,4,256]{2,1,0:T(4,128)}), f32[128,4,256]{2,1,0:T(4,128)S(1)}, u32[]{:S(2)}, u32[]{:S(2)}) %all-to-all-start.7) | async-done | bytes 524320 | tf_op jit(solution)/shard_map/all_to_all | solution.py:19
  213.9 20.4 %while.62 = (s32[]{:T(128)}, f32[1536,256]{1,0:T(8,128)S(1)}, s32[2048]{0:T(1024)S(1)}, s32[2048]{0:T(1024)}, s32[]{:T(128)}, /*index=5*/bf16[1536,256]{1,0:T(8,...) while((s32[]{:T(128)}, f32[1536,256]{1,0:T(8,128)S(1)}, s32[2048]{0:T(1024)S(1)}, ...), condition=%wide.region_5.7_spmd.clone.clone, body=%wide.region_4.6_spmd.clone.clone.sunk | while | flops 808584192 | bytes 3945645 | solution.py:53
  235.4 4.6 %all-to-all-start.5 = ((f32[128,4,256]{2,1,0:T(4,128)}), f32[128,4,256]{2,1,0:T(4,128)S(1)}, u32[]{:S(2)}, u32[]{:S(2)}) async-start(f32[128,4,256]{2,1,0:T(4,128)} %reshape.85), calls=%async_computation.5 | async-start | bytes 1048576 | tf_op jit(solution)/shard_map/all_to_all | solution.py:19
  240.1 30.7 %all-reduce.7.cloned.1.call-done = (f32[256,256]{0,1:T(8,128)}, f32[256,256]{0,1:T(8,128)}, f32[256,256]{0,1:T(8,128)}, f32[256,256]{0,1:T(8,128)}) async-done(((f32[256,256]{0,1:T(8,128)}, f32[256,256]{0,1:T(8,128)}, f32[256,256]{0,1:T(8,128)}, f32[256,256]{0,1:T(8,128)}), (f32[256,256]{0,1:T(8,128)}, f32[256,256]{0,1:T(8,128)}, f32[256,256]{0,1:T(8,128)}, ...) | async-done | bytes 1048592 | tf_op jit(solution)/shard_map/psum | solution.py:121
  270.8 14.3 %psum.78 = f32[256]{0:T(256)S(1)} all-reduce(f32[256]{0:T(256)S(1)} %copy-done.16), channel_id=1, replica_groups=mesh['dom'=16,'sub'=8] {'sub'}, use_global_device_ids=true, to_apply=%region_17.19 | all-reduce | flops 256 | bytes 2048 | tf_op jit(solution)/shard_map/psum | solution.py:121
  285.1 33.5 %psum.79 = f32[256]{0:T(256)S(1)} all-reduce(f32[256]{0:T(256)S(1)} %psum.78), channel_id=1, replica_groups=mesh['dom'=16,'sub'=8] {'dom'}, use_global_device_ids=true, to_apply=%region_18.20 | all-reduce | flops 256 | bytes 2048 | tf_op jit(solution)/shard_map/psum | solution.py:120
  322.9 39.3 %all-reduce.5.cloned.1.call-done = (f32[1,256,256]{1,2,0:T(8,128)}, f32[1,256,256]{1,2,0:T(8,128)}, f32[1,256,256]{1,2,0:T(8,128)}, f32[1,256,256]{1,2,0:T(8,128)}) async-done(((f32[1,256,256]{1,2,0:T(8,128)}, f32[1,256,256]{1,2,0:T(8,128)}, f32[1,256,256]{1,2,0:T(8,128)}, f32[1,256,256]{1,2,0:T(8,128)}), (f32[1,256,256]{1,2,0:T(8,128)}, f32[1,256,256]{1,2,0:T(8,128)}, f32[1,256,256]{1,2,0:T(8,128)}, ...) | async-done | bytes 1048592 | tf_op jit(solution)/shard_map/psum | solution.py:120
  (164 shorter events, 122.9 us)
Async XLA Ops:
  7.2 2.4 copy-start
  10.8 2.0 copy-start.1
  14.8 13.3 %copy-start.12 = (s32[1,128,4]{1,2,0:T(4,128)S(1)}, s32[1,128,4]{1,2,0:T(4,128)}, u32[]{:S(2)}) copy-start(s32[1,128,4]{1,2,0:T(4,128)} %param.30) | copy-start | bytes 6148
  16.2 30.7 %copy-start.9 = (s32[1,2048]{1,0:T(1,128)S(1)}, s32[1,2048]{1,0:T(1,128)}, u32[]{:S(2)}) copy-start(s32[1,2048]{1,0:T(1,128)} %param.31) | copy-start | bytes 24580
  16.2 22.5 %all-to-all-start = ((bf16[128,4,256]{2,1,0:T(4,128)(2,1)}), bf16[128,4,256]{2,1,0:T(4,128)(2,1)}, u32[]{:S(2)}, u32[]{:S(2)}) async-start(bf16[128,4,256]{2,1,0:T(4,128)(2,1)} %get-tuple-element.745), calls=%async_computation | async-start | bytes 524288 | tf_op jit(solution)/shard_map/all_to_all | solution.py:11
  38.7 29.8 %all-to-all-start.2 = ((bf16[128,4,256]{2,1,0:T(4,128)(2,1)}), bf16[128,4,256]{2,1,0:T(4,128)(2,1)S(1)}, u32[]{:S(2)}, u32[]{:S(2)}) async-start(bf16[128,4,256]{2,1,0:T(4,128)(2,1)} %get-tuple-element.744), calls=%async_computation.2 | async-start | bytes 524288 | tf_op jit(solution)/shard_map/all_to_all | solution.py:11
  68.6 34.7 %all-to-all-start.1 = ((f32[128,4,256]{2,1,0:T(4,128)}), f32[128,4,256]{2,1,0:T(4,128)S(1)}, u32[]{:S(2)}, u32[]{:S(2)}) async-start(f32[128,4,256]{2,1,0:T(4,128)} %reshape.79), calls=%async_computation.1 | async-start | bytes 1048576 | tf_op jit(solution)/shard_map/all_to_all | solution.py:19
  101.2 11.8 %copy-start.8 = (bf16[256,256]{1,0:T(8,128)(2,1)S(1)}, bf16[256,256]{1,0:T(8,128)(2,1)}, u32[]{:S(2)}) copy-start(bf16[256,256]{1,0:T(8,128)(2,1)} %param.24) | copy-start | bytes 393220
  103.3 23.4 %all-to-all-start.3 = ((f32[128,4,256]{2,1,0:T(4,128)}), f32[128,4,256]{2,1,0:T(4,128)S(1)}, u32[]{:S(2)}, u32[]{:S(2)}) async-start(f32[128,4,256]{2,1,0:T(4,128)} %reshape.82), calls=%async_computation.3 | async-start | bytes 1048576 | tf_op jit(solution)/shard_map/all_to_all | solution.py:19
  113.1 1.5 copy-start.13
  117.8 12.3 %copy-start.6 = (f32[1024,256]{1,0:T(8,128)S(1)}, f32[1024,256]{1,0:T(8,128)}, u32[]{:S(2)}) copy-start(f32[1024,256]{1,0:T(8,128)} %fusion.82) | copy-start | bytes 3145732
  117.8 12.3 %copy-start.11 = (bf16[256,256]{1,0:T(8,128)(2,1)S(1)}, bf16[256,256]{1,0:T(8,128)(2,1)}, u32[]{:S(2)}) copy-start(bf16[256,256]{1,0:T(8,128)(2,1)} %param.25) | copy-start | bytes 393220
  130.1 1.4 copy-start.5
  138.9 15.6 %all-to-all-start.6 = ((bf16[128,4,256]{2,1,0:T(4,128)(2,1)}), bf16[128,4,256]{2,1,0:T(4,128)(2,1)S(1)}, u32[]{:S(2)}, u32[]{:S(2)}) async-start(bf16[128,4,256]{2,1,0:T(4,128)(2,1)} %get-tuple-element.742), calls=%async_computation.6 | async-start | bytes 524288 | tf_op jit(solution)/shard_map/all_to_all | solution.py:11
  154.6 31.9 %all-to-all-start.4 = ((bf16[128,4,256]{2,1,0:T(4,128)(2,1)}), bf16[128,4,256]{2,1,0:T(4,128)(2,1)S(1)}, u32[]{:S(2)}, u32[]{:S(2)}) async-start(bf16[128,4,256]{2,1,0:T(4,128)(2,1)} %get-tuple-element.743), calls=%async_computation.4 | async-start | bytes 524288 | tf_op jit(solution)/shard_map/all_to_all | solution.py:11
  186.5 23.4 %all-to-all-start.7 = ((f32[128,4,256]{2,1,0:T(4,128)}), f32[128,4,256]{2,1,0:T(4,128)S(1)}, u32[]{:S(2)}, u32[]{:S(2)}) async-start(f32[128,4,256]{2,1,0:T(4,128)} %reshape.88), calls=%async_computation.7 | async-start | bytes 1048576 | tf_op jit(solution)/shard_map/all_to_all | solution.py:19
  196.3 74.5 %all-reduce.7.cloned.1.call-start = ((), (), s32[]{:S(2)}) async-start(), calls=%async_computation.9 | async-start | bytes 2097152 | tf_op jit(solution)/shard_map/psum | solution.py:121
  198.6 11.4 %copy-start.14 = (s32[512]{0:T(512)S(1)}, s32[512]{0:T(512)}, u32[]{:S(2)}) copy-start(s32[512]{0:T(512)} %eq.293) | copy-start | bytes 6148
  212.4 1.5 copy-start.2
  234.3 84.9 %copy-start.3 = (f32[1536,256]{1,0:T(8,128)}, f32[1536,256]{1,0:T(8,128)S(1)}, u32[]{:S(2)}) copy-start(f32[1536,256]{1,0:T(8,128)S(1)} %get-tuple-element.514) | copy-start | bytes 4718596
  234.3 36.5 %copy-start.16 = (f32[256]{0:T(256)S(1)}, f32[256]{0:T(256)}, u32[]{:S(2)}) copy-start(f32[256]{0:T(256)} %get-tuple-element.748) | copy-start | bytes 3076
  235.4 84.0 %copy-start.15 = (s32[512]{0:T(512)S(1)}, s32[512]{0:T(512)}, u32[]{:S(2)}) copy-start(s32[512]{0:T(512)} %eq.293) | copy-start | bytes 6148
  235.4 83.8 %all-to-all-start.5 = ((f32[128,4,256]{2,1,0:T(4,128)}), f32[128,4,256]{2,1,0:T(4,128)S(1)}, u32[]{:S(2)}, u32[]{:S(2)}) async-start(f32[128,4,256]{2,1,0:T(4,128)} %reshape.85), calls=%async_computation.5 | async-start | bytes 1048576 | tf_op jit(solution)/shard_map/all_to_all | solution.py:19
  240.0 122.1 %all-reduce.5.cloned.1.call-start = ((), (), s32[]{:S(2)}) async-start(), calls=%async_computation.8 | async-start | bytes 2097152 | tf_op jit(solution)/shard_map/psum | solution.py:120
  (4 other events, 5.3 us)
Sparse Core Ops, SparseCore 0:
  213.6 57.0 all-reduce.6
  274.4 87.7 all-reduce.4
